TPU v7x, 128 devices: a whole 4x4x4 slice. The times are simulated.
128 devices in a mesh: row: 16 (over z, x_lo, core), col: 8 (over x_hi, y).
Axes of the slice: x: 4 (x_hi: 2, x_lo: 2; x = x_hi * 2 + x_lo), y: 4, z: 4, core: 2. Of those that a mesh axis runs over, the one named last changes fastest.
Arguments:
- base_weight: bfloat16 [16384, 49152], P('row', 'col'), may hold values from -6 to 6
- left_factor: float32 [16384, 256], P('row', 'col'), may hold values from -6 to 6
- right_factor: float32 [256, 49152], P('row', 'col'), may hold values from -0.375 to 0.375
Outputs:
- merged: bfloat16 [16384, 49152], P(None, ('row', 'col'))
All inputs are finite; a program needn't handle non-finite values.
Results may differ from a plain program's by a relative error of at most 0.001.
Values may be sent and summed in bfloat16 or wider, within the bound.
No kernel may reach another device: no remote copies, remote signals or barrier semaphores. Data moves between devices by JAX's collectives and lax.ppermute only.
A program may use at most 192 MiB of HBM per device.

v0:
```python
import jax
import jax.numpy as jnp
from jax import lax
from jax.sharding import PartitionSpec as P


def copy_for_each(value, axis):
    length = lax.axis_size(axis)
    return lax.all_to_all(
        jnp.broadcast_to(value[None], (length, *value.shape)), axis, 0, 0, tiled=True
    )


def joined_along(tiles, dim):
    tiles = jnp.moveaxis(tiles, 0, dim)
    lengths = tiles.shape
    return tiles.reshape(*lengths[:dim], lengths[dim] * lengths[dim + 1], *lengths[dim + 2 :])


def gathered_copies(value, axis, dim):
    tiles = copy_for_each(value, axis)
    return joined_along(tiles, dim)


def to_serving(stored):
    row_count = lax.axis_size("row")
    col_count = lax.axis_size("col")
    height = stored.shape[0]
    block_width = stored.shape[1] // row_count
    group_count = row_count // col_count
    shaped = stored.reshape(height, group_count, col_count, block_width)
    across = lax.all_to_all(shaped, "col", split_axis=2, concat_axis=1, tiled=True)
    served = lax.all_to_all(across, "row", split_axis=1, concat_axis=0, tiled=True)
    return served.reshape(height * row_count, block_width)


def body(base_weight, left_factor, right_factor):
    left_cols = gathered_copies(left_factor, "col", 1)
    delta = jnp.dot(
        left_cols,
        lax.all_gather(right_factor, "row", axis=0, tiled=True),
        precision=lax.Precision.HIGHEST,
        preferred_element_type=jnp.float32,
    )
    merged_block = (base_weight.astype(jnp.float32) + delta).astype(jnp.bfloat16)
    return to_serving(merged_block)


def solution(mesh):
    placed = (P("row", "col"), P("row", "col"), P("row", "col"))
    return jax.shard_map(
        body, mesh=mesh, in_specs=placed, out_specs=P(None, ("row", "col")), check_vma=False
    )
```

profile of v0, /device:TPU:1, one launch (start us, length us, event | category | flops | bytes accessed | tf_op | source)
XLA Modules:
  0.0 399.2 jit_solution(9621992016833128022)
XLA Ops:
  6.5 0.0 all-gather.2.cloned.1.call-start
  6.5 0.7 all-gather.2.cloned.1.call-update
  7.3 1.0 broadcast_in_dim.2
  8.3 26.6 %all_to_all.38 = f32[8,1024,32]{1,2,0:T(8,128)S(1)} all-to-all(f32[8,1024,32]{1,2,0:T(8,128)S(1)} %broadcast_in_dim.2), channel_id=1, replica_groups=mesh['row'=16,'col'=8] {'col'}, dimensions={0} | all-to-all | bytes 2097152 | tf_op jit(solution)/shard_map/all_to_all | solution.py:9
  34.9 25.6 %all-gather.2.cloned.1.call-done = f32[256,6144]{1,0:T(8,128)} async-done(((f32[16,6144]{1,0:T(8,128)}), f32[256,6144]{1,0:T(8,128)}) %all-gather.2.cloned.1.call-update) | async-done | bytes 6291472 | tf_op jit(solution)/shard_map/all_gather | solution.py:41
  60.4 23.9 %add_convert_fusion = bf16[1024,6144]{1,0:T(8,128)(2,1)S(1)} fusion(bf16[1024,6144]{1,0:T(8,128)(2,1)} %param.3, f32[1024,256]{0,1:T(8,128)S(1)} %bitcast.24, f32[256,6144]{1,0:T(8,128)} %all-gather.2.cloned.1.call-done), kind=kOutput, calls=%fused_computation | convolution fusion | flops 19346227200 | bytes 32505856 | tf_op jit(solution)/shard_map/dot_general | solution.py:39
  84.3 3.0 copy.8
  87.3 7.9 %copy.6 = bf16[1024,2,8,384]{3,0,1,2:T(8,128)(2,1)S(1)} copy(bf16[1024,2,8,384]{3,2,1,0:T(8,128)(2,1)S(1)} %bitcast.21) | data formatting | bytes 25165824 | tf_op jit(solution)/shard_map/reshape | solution.py:31
  95.2 146.6 %all_to_all.39 = bf16[1024,2,8,384]{3,0,1,2:T(8,128)(2,1)S(1)} all-to-all(bf16[1024,2,8,384]{3,0,1,2:T(8,128)(2,1)S(1)} %copy.6), channel_id=1, replica_groups=mesh['row'=16,'col'=8] {'col'}, dimensions={2} | all-to-all | bytes 25165824 | tf_op jit(solution)/shard_map/all_to_all | solution.py:32
  241.9 145.6 %all_to_all.40 = bf16[1024,16,1,384]{3,0,2,1:T(8,128)(2,1)S(1)} all-to-all(bf16[1024,16,1,384]{3,0,2,1:T(8,128)(2,1)S(1)} %bitcast.22), channel_id=1, replica_groups=mesh['row'=16,'col'=8] {'row'}, dimensions={1} | all-to-all | bytes 25165824 | tf_op jit(solution)/shard_map/all_to_all | solution.py:33
  387.5 4.8 %copy.10 = bf16[16384,384]{1,0:T(8,128)(2,1)} copy(bf16[16384,384]{1,0:T(8,128)(2,1)S(1)} %bitcast.23) | data formatting | bytes 25165824
Async XLA Ops:
  6.5 53.9 %all-gather.2.cloned.1.call-start = ((), (), s32[]{:S(2)}) async-start(), calls=%async_computation.3 | async-start | bytes 6684672 | tf_op jit(solution)/shard_map/all_gather | solution.py:41
Sparse Core Ops, SparseCore 0:
  9.1 51.3 all-gather.1
where the time goes:
time: 399 us
  blocking collectives  319 us (80%)
  waiting for transfers between devices  26.3 us (7%)
  matrix products  23.9 us (6%)
  local copies, waits for them, and re-layouts  16.7 us (4%)
  between operations  13.4 us (3%)
    all_to_all x1, blocking collectives, to_serving(): lax.all_to_all(shaped, 'col', split_axis=2, concat_axis=1, tiled=True)  147 us
    all_to_all x1, blocking collectives, to_serving(): lax.all_to_all(across, 'row', split_axis=1, concat_axis=0, tiled=True)  146 us
    all_to_all x1, blocking collectives, copy_for_each(): lax.all_to_all(jnp.broadcast_to(value[None], (length, *value.shape)), axi...  26.6 us
    all_gather x1, waiting for transfers between devices, body(): lax.all_gather(right_factor, 'row', axis=0, tiled=True)  25.6 us
    dot_general x1, matrix products, body(): jnp.dot(left_cols, lax.all_gather(right_factor, 'row', axis=0, tiled=True...  23.9 us
  transfers between devices with their start and end apart: 1, of which 1 were waited for; matrix products, arithmetic and copies ran while one was open for 0% of the time, Pallas kernels for 0%

commit v1 on v0

--- a/solution.py
+++ b/solution.py
@@ -38,7 +38,9 @@
     left_cols = gathered_copies(left_factor, "col", 1)
     delta = jnp.dot(
         left_cols,
-        lax.all_gather(right_factor, "row", axis=0, tiled=True),
+        jnp.concatenate(
+            lax.all_to_all(jnp.stack([right_factor] * lax.axis_size("row")), "row", 0, 0), axis=0
+        ),
         precision=lax.Precision.HIGHEST,
         preferred_element_type=jnp.float32,
     )

time: 399 us -> 432 us (1.083)
  blocking collectives: 319 us -> 389 us
  waiting for transfers between devices: 26.3 us -> 0 us
  between operations: 13.4 us -> 0.04 us
    all_to_all x0 -> x1, blocking collectives: none -> 79.3 us  [body(): lax.all_to_all(jnp.stack([right_factor] * lax.axis_size('row')), 'row', 0...]
    all_gather x1 -> x0, waiting for transfers between devices: 25.6 us -> none  [body(): lax.all_gather(right_factor, 'row', axis=0, tiled=True)]
    all_to_all x1, blocking collectives: 147 us -> 141 us  [to_serving(): lax.all_to_all(shaped, 'col', split_axis=2, concat_axis=1, tiled=True)]
  transfers between devices with their start and end apart: 1 -> 0, of which waited for: 1 -> 0; matrix products, arithmetic and copies ran while one was open for 0% -> 0% of each run, Pallas kernels for 0% -> 0%
where the time goes in v1:
time: 432 us; the launch traced here: 431 us
  blocking collectives  389 us (90%)
  matrix products  23.9 us (6%)
  local copies, waits for them, and re-layouts  18.4 us (4%)
    all_to_all x1, blocking collectives, to_serving(): lax.all_to_all(across, 'row', split_axis=1, concat_axis=0, tiled=True)  146 us
    all_to_all x1, blocking collectives, to_serving(): lax.all_to_all(shaped, 'col', split_axis=2, concat_axis=1, tiled=True)  141 us
    all_to_all x1, blocking collectives, body(): lax.all_to_all(jnp.stack([right_factor] * lax.axis_size('row')), 'row', 0...  79.3 us
    dot_general x1, matrix products, body(): jnp.dot(left_cols, jnp.concatenate(lax.all_to_all(jnp.stack([right_factor...  23.9 us
    all_to_all x1, blocking collectives, copy_for_each(): lax.all_to_all(jnp.broadcast_to(value[None], (length, *value.shape)), axi...  22.9 us

profile of v1, /device:TPU:1, one launch (start us, length us, event | category | flops | bytes accessed | tf_op | source)
XLA Modules:
  0.0 431.4 jit_solution(8993340598130317654)
XLA Ops:
  0.0 1.0 broadcast_in_dim.2
  1.0 22.9 %all_to_all.43 = f32[8,1024,32]{1,2,0:T(8,128)S(1)} all-to-all(f32[8,1024,32]{1,2,0:T(8,128)S(1)} %broadcast_in_dim.2), channel_id=1, replica_groups=mesh['row'=16,'col'=8] {'col'}, dimensions={0} | all-to-all | bytes 2097152 | tf_op jit(solution)/shard_map/all_to_all | solution.py:9
  23.9 1.7 stack.2
  25.6 79.3 %all_to_all.44 = f32[16,16,6144]{2,1,0:T(8,128)S(1)} all-to-all(f32[16,16,6144]{2,1,0:T(8,128)S(1)} %stack.2), channel_id=1, replica_groups=mesh['row'=16,'col'=8] {'row'}, dimensions={0} | all-to-all | bytes 12582912 | tf_op jit(solution)/shard_map/all_to_all | solution.py:42
  104.9 23.9 %add_convert_fusion = bf16[1024,6144]{1,0:T(8,128)(2,1)S(1)} fusion(bf16[1024,6144]{1,0:T(8,128)(2,1)} %param.3, f32[1024,256]{0,1:T(8,128)S(1)} %bitcast.26, f32[256,6144]{1,0:T(8,128)S(1)} %bitcast.25), kind=kOutput, calls=%fused_computation | convolution fusion | flops 19346227200 | bytes 32505856 | tf_op jit(solution)/shard_map/dot_general | solution.py:39
  128.8 3.0 copy.8
  131.8 7.9 %copy.6 = bf16[1024,2,8,384]{3,0,1,2:T(8,128)(2,1)S(1)} copy(bf16[1024,2,8,384]{3,2,1,0:T(8,128)(2,1)S(1)} %bitcast.22) | data formatting | bytes 25165824 | tf_op jit(solution)/shard_map/reshape | solution.py:31
  139.7 141.2 %all_to_all.45 = bf16[1024,2,8,384]{3,0,1,2:T(8,128)(2,1)S(1)} all-to-all(bf16[1024,2,8,384]{3,0,1,2:T(8,128)(2,1)S(1)} %copy.6), channel_id=1, replica_groups=mesh['row'=16,'col'=8] {'col'}, dimensions={2} | all-to-all | bytes 25165824 | tf_op jit(solution)/shard_map/all_to_all | solution.py:32
  280.9 145.7 %all_to_all.46 = bf16[1024,16,1,384]{3,0,2,1:T(8,128)(2,1)S(1)} all-to-all(bf16[1024,16,1,384]{3,0,2,1:T(8,128)(2,1)S(1)} %bitcast.23), channel_id=1, replica_groups=mesh['row'=16,'col'=8] {'row'}, dimensions={1} | all-to-all | bytes 25165824 | tf_op jit(solution)/shard_map/all_to_all | solution.py:33
  426.6 4.8 %copy.10 = bf16[16384,384]{1,0:T(8,128)(2,1)} copy(bf16[16384,384]{1,0:T(8,128)(2,1)S(1)} %bitcast.24) | data formatting | bytes 25165824
